TPU v7x, 512 devices: a whole 4x4x16 slice. The times are simulated.
512 devices in a mesh: gx: 32 (over z_lo, y, core), gy: 16 (over x, z_hi).
Axes of the slice: x: 4, y: 4, z: 16 (z_hi: 4, z_lo: 4; z = z_hi * 4 + z_lo), core: 2. Of those that a mesh axis runs over, the one named last changes fastest.
Arguments:
- deflation: float32 [32, 320, 80, 128], P(None, 'gx', 'gy'), may hold values from -13 to 13
- layers: int32 [256, 48, 128], P('gx', 'gy'), may hold values from 0 to 84
- layer_table: float32 [85], replicated, may hold values from 0.02 to 2
- forcing: float32 [256, 48, 128], P('gx', 'gy'), may hold values from -13 to 13
Outputs:
- coarse_rows: float32 [32, 16, 9, 32, 32], P('gx', 'gy')
- coarse_solution: float32 [32, 16, 32], P('gx', 'gy')
All inputs are finite; a program needn't handle non-finite values.
Results may differ from a plain program's by a relative error of at most 0.0003.
Values sent between devices are 32-bit elements; how exact they have to be, the bound alone decides.
A program may use at most 64 MiB of HBM per device.

v0:
```python
import math
import jax
import jax.numpy as jnp
from jax import lax
from jax.sharding import PartitionSpec as P

VEC = 32
CX = 8
CY = 3
CZ = 128
MARGIN = 1
LAYERS = 85
ITERS = 3
EX = 10
EY = 5
storage_term = 0.5
upper_offsets = ((0, 0), (0, 1), (1, -1), (1, 0), (1, 1))


def extended(value, sides, width):
    for axis, dim in sides:
        devices, length = (lax.axis_size(axis), value.shape[dim])
        up = [(i, (i + 1) % devices) for i in range(devices - 1)]
        down = [(j, i) for i, j in up]
        last = lax.slice_in_dim(value, length - width, length, axis=dim)
        initial = lax.slice_in_dim(value, 0, width, axis=dim)
        before = lax.ppermute(last, axis, up)
        after = lax.ppermute(initial, axis, down)
        value = jnp.concatenate([before, value, after], axis=dim)
    return value


def unity_weights(index_pos, subdomains, own_cells):
    offset = jnp.arange(own_cells + 2 * MARGIN, dtype=jnp.int32)
    global_pos = index_pos * own_cells - MARGIN + offset
    inside = ((global_pos >= 0) & (global_pos < subdomains * own_cells)).astype(jnp.float32)
    below_side = ((index_pos > 0) & (global_pos < index_pos * own_cells + MARGIN)).astype(
        jnp.float32
    )
    above_side = (
        (index_pos < subdomains - 1) & (global_pos >= (index_pos + 1) * own_cells - MARGIN)
    ).astype(jnp.float32)
    return inside / (1.0 + below_side + above_side)


def operate(padded, kappa_box):
    centre = padded[:, 1:-1, 1:-1]
    kappa_centre = kappa_box[1:-1, 1:-1]
    width_x = centre.shape[1]
    width_y = centre.shape[2]
    result = storage_term * centre
    for shift_x, shift_y in ((1, 0), (-1, 0), (0, 1), (0, -1)):
        beside = padded[:, 1 + shift_x : 1 + shift_x + width_x, 1 + shift_y : 1 + shift_y + width_y]
        kappa_beside = kappa_box[
            1 + shift_x : 1 + shift_x + width_x, 1 + shift_y : 1 + shift_y + width_y
        ]
        result = result + jnp.sqrt(kappa_centre * kappa_beside) * (centre - beside)
    for forward in (True, False):
        if forward:
            beside = jnp.pad(centre[..., 1:], ((0, 0), (0, 0), (0, 0), (0, 1)))
            kappa_beside = jnp.pad(kappa_centre[..., 1:], ((0, 0), (0, 0), (0, 1)))
        else:
            beside = jnp.pad(centre[..., :-1], ((0, 0), (0, 0), (0, 0), (1, 0)))
            kappa_beside = jnp.pad(kappa_centre[..., :-1], ((0, 0), (0, 0), (1, 0)))
        result = result + jnp.sqrt(kappa_centre * kappa_beside) * (centre - beside)
    return result


def strip_bounds(shift, ext_cells):
    slab_depth = 2 * MARGIN + 1
    if shift < 0:
        return (0, 0, slab_depth)
    if shift == 0:
        return (slab_depth, 1, ext_cells)
    return (slab_depth + ext_cells, ext_cells + 2 - slab_depth, slab_depth)


def block_with(applied, strip, shift_x, shift_y):
    unused_x, start_bx, length_x = strip_bounds(shift_x, EX)
    unused_y, start_by, length_y = strip_bounds(shift_y, EY)
    region = applied[:, start_bx : start_bx + length_x, start_by : start_by + length_y]
    return jnp.dot(
        region.reshape(VEC, -1), strip.reshape(VEC, -1).T, precision=lax.Precision.HIGHEST
    )


def conjugate(coarse_load, image_of, total_of):
    solution = jnp.zeros_like(coarse_load)
    residual = coarse_load
    direction = coarse_load
    norm_now = total_of(jnp.sum(residual * residual))
    for iteration in range(ITERS):
        mapped = image_of(direction)
        step_size = norm_now / total_of(jnp.sum(direction * mapped))
        solution = solution + step_size * direction
        residual = residual - step_size * mapped
        norm_next = total_of(jnp.sum(residual * residual))
        direction = residual + norm_next / norm_now * direction
        norm_now = norm_next
    return solution


def plain_total(value):
    return value


def take_from(vector, offset, reach):
    count = vector.shape[1]
    padded_vec = jnp.pad(vector, ((0, 0), (reach, reach)))
    return padded_vec[:, reach + offset : reach + offset + count]


def half_product(upper_rows, vector, mesh_x, mesh_y):
    count = vector.shape[1]
    reach = mesh_y + 1
    flat = jnp.arange(count, dtype=jnp.int32)
    place_x = flat // mesh_y
    place_y = flat % mesh_y
    result = jnp.zeros_like(vector)
    spread = jnp.zeros_like(vector)
    for slot_index in range(len(upper_offsets)):
        shift_x, shift_y = upper_offsets[slot_index]
        offset = shift_x * mesh_y + shift_y
        valid = (
            (place_x + shift_x >= 0)
            & (place_x + shift_x < mesh_x)
            & (place_y + shift_y >= 0)
            & (place_y + shift_y < mesh_y)
        ).astype(jnp.float32)
        coarse_block = upper_rows[slot_index]
        moved = take_from(vector, offset, reach) * valid[None, :]
        result = result + jnp.sum(coarse_block * moved[None, :, :], axis=1)
        if shift_x != 0 or shift_y != 0:
            sent_back = jnp.sum(coarse_block * vector[:, None, :], axis=0) * valid[None, :]
            spread = spread + take_from(sent_back, -offset, reach)
    return result + spread


def body(deflation, layers, layer_table, forcing):
    mesh_x = lax.axis_size("gx")
    mesh_y = lax.axis_size("gy")
    index_x = lax.axis_index("gx")
    index_y = lax.axis_index("gy")
    slab_depth = 2 * MARGIN + 1
    onehot = (layers.reshape(1, -1) == jnp.arange(LAYERS, dtype=jnp.int32)[:, None]).astype(
        jnp.float32
    )
    permeability = jnp.dot(layer_table, onehot, precision=lax.Precision.HIGHEST).reshape(CX, CY, CZ)
    fields = jnp.stack([permeability, forcing])
    rimmed = extended(fields, (("gx", 1), ("gy", 2)), MARGIN + 1)
    weights = (
        unity_weights(index_x, mesh_x, CX)[:, None, None]
        * unity_weights(index_y, mesh_y, CY)[None, :, None]
    )
    basis = deflation * weights * (1.0 / math.sqrt(CX * CY * CZ))
    kappa_box = jnp.pad(rimmed[0], ((1, 1), (1, 1), (0, 0)))
    forcing_ext = rimmed[1, 1:-1, 1:-1]
    applied = operate(jnp.pad(basis, ((0, 0), (2, 2), (2, 2), (0, 0))), kappa_box)
    coarse_load = jnp.dot(
        basis.reshape(VEC, -1), forcing_ext.reshape(-1), precision=lax.Precision.HIGHEST
    )
    beside_all = extended(basis, (("gx", 1), ("gy", 2)), slab_depth)
    blocks = []
    for shift_x in (-1, 0, 1):
        for shift_y in (-1, 0, 1):
            start_nx, unused_bx, length_x = strip_bounds(shift_x, EX)
            start_ny, unused_by, length_y = strip_bounds(shift_y, EY)
            strip = beside_all[:, start_nx : start_nx + length_x, start_ny : start_ny + length_y]
            blocks.append(block_with(applied, strip, shift_x, shift_y))
    coarse_rows = jnp.stack(blocks)
    gathered_rows, gathered_load = (
        lax.all_gather(coarse_rows[4:].reshape(1, 5 * VEC * VEC), ("gx", "gy"), axis=0, tiled=True),
        lax.all_gather(coarse_load.reshape(1, VEC), ("gx", "gy"), axis=0, tiled=True),
    )
    upper_rows = gathered_rows.T.reshape(5, VEC, VEC, mesh_x * mesh_y)
    whole_load = gathered_load.T

    def image_all(vector):
        return half_product(upper_rows, vector, mesh_x, mesh_y)

    whole_solution = conjugate(whole_load, image_all, plain_total)
    flat_index = index_x * mesh_y + index_y
    solution = lax.dynamic_slice(whole_solution, (jnp.int32(0), flat_index), (VEC, 1)).reshape(
        1, 1, VEC
    )
    return (coarse_rows[None, None], solution)


def solution(mesh):
    return jax.shard_map(
        body,
        mesh=mesh,
        in_specs=(P(None, "gx", "gy", None), P("gx", "gy", None), P(), P("gx", "gy", None)),
        out_specs=(P("gx", "gy", None, None, None), P("gx", "gy", None)),
        check_vma=False,
    )
```

profile of v0, /device:TPU:99, one launch (start us, length us, event | category | flops | bytes accessed | tf_op | source)
XLA Modules:
  0.0 2032.0 jit_solution(9259440537845964551)
XLA Ops:
  9.2 2.6 collective-permute-start.1
  11.7 3.1 collective-permute-start
  15.0 1.3 multiply_multiply_fusion
  17.1 2.7 collective-permute-start.5
  19.8 2.8 collective-permute-start.4
  23.4 9.7 collective-permute-start.3
  33.1 1.9 collective-permute-start.2
  35.0 1.5 pad_slice_fusion.1
  37.1 1.2 reshape.203
  38.2 4.6 collective-permute-done.2
  43.6 1.9 convolution_bitcast_fusion.9
  47.3 1.2 pad_maximum_fusion
  48.7 2.1 collective-permute-start.6
  51.0 8.2 collective-permute-start.7
  59.2 1.1 fusion.7
  60.3 64.6 %collective-permute-done.6 = f32[32,16,3,128]{3,0,2,1:T(8,128)S(1)} collective-permute-done((f32[32,16,3,128]{3,0,2,1:T(8,128)S(1)}, f32[32,16,3,128]{3,0,2,1:T(8,128)S(1)}, u32[]{:S(2)}, u32[]{:S(2)}) %collective-permute-start.6) | collective-permute-done | bytes 786464 | tf_op jit(solution)/shard_map/ppermute | solution.py:27
  125.1 1.3 fusion.16
  128.9 1.3 constant_dynamic-update-slice_fusion.6
  131.2 402.9 %all-reduce.24.cloned.1.call-done = f32[16384]{0:T(1024)} async-done(((f32[16384]{0:T(1024)}), f32[16384]{0:T(1024)}) %all-reduce.24.cloned.1.call-update) | async-done | bytes 65552
  534.2 0.9 reshape.207
  535.3 1425.0 %all-gather.4.cloned.1.call-done = f32[512,1,5120]{2,1,0:T(1,128)} async-done(((f32[1,1,5120]{2,1,0:T(1,128)}), f32[512,1,5120]{2,1,0:T(1,128)}) %all-gather.4.cloned.1.call-update) | async-done | bytes 10485776 | tf_op jit(solution)/shard_map/all_gather | solution.py:172
  1960.3 22.0 %copy.43 = f32[512,1,5120]{0,2,1:T(8,128)} copy(f32[512,1,5120]{2,1,0:T(1,128)} %all-gather.4.cloned.1.call-done) | data formatting | bytes 20971520 | tf_op jit(solution)/shard_map/all_gather | solution.py:172
  1982.3 4.7 fusion.83
  1987.0 1.1 multiply_reduce_fusion.18
  1988.3 0.8 copy-done.2
  1989.1 1.0 copy-done.3
  1990.3 1.3 slice-done.2
  1991.5 2.1 multiply_reduce_fusion.25
  1997.6 4.1 multiply_reduce_fusion.9
  2001.8 6.3 multiply_reduce_fusion.16
  2011.9 4.1 multiply_reduce_fusion
  2016.1 6.3 multiply_reduce_fusion.7
  (76 shorter events, 15.6 us)
Async XLA Ops:
  7.2 1.5 copy-start
  7.2 527.0 %all-reduce.24.cloned.1.call-start = ((), (), s32[]{:S(2)}) async-start(), calls=%async_computation | async-start | bytes 131072
  9.2 13.5 collective-permute-start.1
  11.7 10.9 collective-permute-start
  17.1 30.2 %collective-permute-start.5 = (f32[32,3,5,128]{3,0,2,1:T(8,128)}, f32[32,3,5,128]{3,0,2,1:T(8,128)}, u32[]{:S(2)}, u32[]{:S(2)}) collective-permute-start(f32[32,3,5,128]{3,0,2,1:T(8,128)} %get-tuple-element.47), channel_id=1, source_target_pairs={{16,0},{32,16},{48,32},{64,48},{80,64},{96,80},{112,96},{128,112},... | collective-permute-start | bytes 737288 | tf_op jit(solution)/shard_map/ppermute | solution.py:28
  19.8 27.5 %collective-permute-start.4 = (f32[32,3,5,128]{3,0,2,1:T(8,128)}, f32[32,3,5,128]{3,0,2,1:T(8,128)}, u32[]{:S(2)}, u32[]{:S(2)}) collective-permute-start(f32[32,3,5,128]{3,0,2,1:T(8,128)} %get-tuple-element.46), channel_id=1, source_target_pairs={{0,16},{16,32},{32,48},{48,64},{64,80},{80,96},{96,112},{112,128},... | collective-permute-start | bytes 737288 | tf_op jit(solution)/shard_map/ppermute | solution.py:27
  22.7 10.4 copy-start.6
  23.4 14.9 collective-permute-start.3
  33.1 9.7 collective-permute-start.2
  45.8 0.6 copy-start.5
  46.4 1913.9 %all-gather.4.cloned.1.call-start = ((), (), s32[]{:S(2)}) async-start(), calls=%async_computation.1 | async-start | bytes 10506240 | tf_op jit(solution)/shard_map/all_gather | solution.py:172
  48.5 10.6 copy-start.4
  48.7 76.1 %collective-permute-start.6 = (f32[32,16,3,128]{3,0,2,1:T(8,128)S(1)}, f32[32,16,3,128]{3,0,2,1:T(8,128)S(1)}, u32[]{:S(2)}, u32[]{:S(2)}) collective-permute-start(f32[32,16,3,128]{3,0,2,1:T(8,128)S(1)} %get-tuple-element.45), channel_id=1, source_target_pairs={{0,1},{1,2},{2,3},{3,4},{4,5},{5,6},{6,7},{7,8},{8,9},{9,10},{10,1... | collective-permute-start | bytes 2359304 | tf_op jit(solution)/shard_map/ppermute | solution.py:27
  51.0 75.5 %collective-permute-start.7 = (f32[32,16,3,128]{3,0,2,1:T(8,128)S(1)}, f32[32,16,3,128]{3,0,2,1:T(8,128)S(1)}, u32[]{:S(2)}, u32[]{:S(2)}) collective-permute-start(f32[32,16,3,128]{3,0,2,1:T(8,128)S(1)} %get-tuple-element.44), channel_id=1, source_target_pairs={{1,0},{2,1},{3,2},{4,3},{5,4},{6,5},{7,6},{8,7},{9,8},{10,9},{11,1... | collective-permute-start | bytes 2359304 | tf_op jit(solution)/shard_map/ppermute | solution.py:28
  130.5 1851.8 %copy-start.7 = (f32[9,32,32]{2,1,0:T(8,128)}, f32[9,32,32]{2,1,0:T(8,128)S(1)}, u32[]{:S(2)}) copy-start(f32[9,32,32]{2,1,0:T(8,128)S(1)} %get-tuple-element.75) | copy-start | bytes 110596
  1982.3 8.0 slice-start
  1982.3 8.0 slice-start.1
  1987.0 1.3 copy-start.1
  1987.0 2.1 copy-start.2
  1987.0 3.1 copy-start.3
  1987.0 4.5 slice-start.2
Sparse Core Ops, SparseCore 0:
  46.5 487.5 all-reduce.23
  536.7 1423.5 all-gather.3
where the time goes:
time: 2030 us
  waiting for transfers between devices  1900 us (94%)
  local copies, waits for them, and re-layouts  39 us (2%)
  other arithmetic  33.9 us (2%)
  starting transfers between devices  33.2 us (2%)
  between operations  20.8 us (1%)
    all_gather x1, waiting for transfers between devices, body(): lax.all_gather(coarse_rows[4:].reshape(1, 5 * VEC * VEC), ('gx', 'gy'), a...  1430 us
    unnamed x3, waiting for transfers between devices  403 us
    ppermute x4, waiting for transfers between devices, extended(): before = lax.ppermute(last, axis, up)  69.1 us
  transfers between devices with their start and end apart: 10, of which 4 were waited for; matrix products, arithmetic and copies ran while one was open for 1% of the time, Pallas kernels for 0%

commit v1 on v0

--- a/solution.py
+++ b/solution.py
@@ -169,7 +169,17 @@
             blocks.append(block_with(applied, strip, shift_x, shift_y))
     coarse_rows = jnp.stack(blocks)
     gathered_rows, gathered_load = (
-        lax.all_gather(coarse_rows[4:].reshape(1, 5 * VEC * VEC), ("gx", "gy"), axis=0, tiled=True),
+        jnp.concatenate(
+            lax.all_to_all(
+                jnp.stack(
+                    [coarse_rows[4:].reshape(1, 5 * VEC * VEC)] * lax.axis_size(("gx", "gy"))
+                ),
+                ("gx", "gy"),
+                0,
+                0,
+            ),
+            axis=0,
+        ),
         lax.all_gather(coarse_load.reshape(1, VEC), ("gx", "gy"), axis=0, tiled=True),
     )
     upper_rows = gathered_rows.T.reshape(5, VEC, VEC, mesh_x * mesh_y)

time: 2030 us -> 780 us (0.38)
  the two profiles are of different devices: /device:TPU:99 before, /device:TPU:1 now
where the time goes in v1:
time: 780 us; the launch traced here: 779 us
  waiting for transfers between devices  624 us (80%)
  starting transfers between devices  56.5 us (7%)
  local copies, waits for them, and re-layouts  41.7 us (5%)
  other arithmetic  31.3 us (4%)
  between operations  20.8 us (3%)
    unnamed x2, waiting for transfers between devices  551 us
    ppermute x4, waiting for transfers between devices, extended(): after = lax.ppermute(initial, axis, down)  47.2 us
    ppermute x4, waiting for transfers between devices, extended(): before = lax.ppermute(last, axis, up)  25.7 us
    all_to_all x1, local copies, waits for them, and re-layouts, body(): lax.all_to_all(jnp.stack([coarse_rows[4:].reshape(1, 5 * VEC * VEC)] * la...  22 us
    all_to_all x1, starting transfers between devices, body(): lax.all_to_all(jnp.stack([coarse_rows[4:].reshape(1, 5 * VEC * VEC)] * la...  21.7 us
    ppermute x4, starting transfers between devices, extended(): before = lax.ppermute(last, axis, up)  21 us
  transfers between devices with their start and end apart: 10, of which 4 were waited for; matrix products, arithmetic and copies ran while one was open for 1% of the time, Pallas kernels for 0%

profile of v1, /device:TPU:1, one launch (start us, length us, event | category | flops | bytes accessed | tf_op | source)
XLA Modules:
  0.0 779.0 jit_solution(660774061685813022)
XLA Ops:
  9.1 8.8 %collective-permute-start.1 = (f32[2,2,3,128]{3,2,1,0:T(4,128)S(1)}, f32[2,2,3,128]{3,2,1,0:T(4,128)S(1)}, u32[]{:S(2)}, u32[]{:S(2)}) collective-permute-start(f32[2,2,3,128]{3,2,1,0:T(4,128)S(1)} %get-tuple-element.73), channel_id=1, source_target_pairs={{16,0},{32,16},{48,32},{64,48},{80,64},{96,80},{112,96},{128,112},... | collective-permute-start | bytes 18440 | tf_op jit(solution)/shard_map/ppermute | solution.py:28
  17.9 1.9 collective-permute-start
  20.0 1.3 multiply_multiply_fusion
  21.3 2.4 collective-permute-start.5
  23.7 3.2 collective-permute-start.4
  27.0 1.3 collective-permute-start.3
  28.3 7.9 %collective-permute-start.2 = (f32[2,12,2,128]{3,2,1,0:T(2,128)S(1)}, f32[2,12,2,128]{3,2,1,0:T(2,128)S(1)}, u32[]{:S(2)}, u32[]{:S(2)}) collective-permute-start(f32[2,12,2,128]{3,2,1,0:T(2,128)S(1)} %get-tuple-element.70), channel_id=1, source_target_pairs={{0,1},{1,2},{2,3},{3,4},{4,5},{5,6},{6,7},{7,8},{8,9},{9,10},{10,1... | collective-permute-start | bytes 73736 | tf_op jit(solution)/shard_map/ppermute | solution.py:27
  37.5 8.1 %collective-permute-start.6 = (f32[32,16,3,128]{3,0,2,1:T(8,128)S(1)}, f32[32,16,3,128]{3,0,2,1:T(8,128)S(1)}, u32[]{:S(2)}, u32[]{:S(2)}) collective-permute-start(f32[32,16,3,128]{3,0,2,1:T(8,128)S(1)} %get-tuple-element.45), channel_id=1, source_target_pairs={{0,1},{1,2},{2,3},{3,4},{4,5},{5,6},{6,7},{7,8},{8,9},{9,10},{10,1... | collective-permute-start | bytes 2359304 | tf_op jit(solution)/shard_map/ppermute | solution.py:27
  45.8 1.3 collective-permute-start.7
  47.1 1.1 fusion.7
  48.2 25.2 %collective-permute-done.6 = f32[32,16,3,128]{3,0,2,1:T(8,128)S(1)} collective-permute-done((f32[32,16,3,128]{3,0,2,1:T(8,128)S(1)}, f32[32,16,3,128]{3,0,2,1:T(8,128)S(1)}, u32[]{:S(2)}, u32[]{:S(2)}) %collective-permute-start.6) | collective-permute-done | bytes 786464 | tf_op jit(solution)/shard_map/ppermute | solution.py:27
  74.0 47.2 %collective-permute-done.7 = f32[32,16,3,128]{3,0,2,1:T(8,128)S(1)} collective-permute-done((f32[32,16,3,128]{3,0,2,1:T(8,128)S(1)}, f32[32,16,3,128]{3,0,2,1:T(8,128)S(1)}, u32[]{:S(2)}, u32[]{:S(2)}) %collective-permute-start.7) | collective-permute-done | bytes 786464 | tf_op jit(solution)/shard_map/ppermute | solution.py:28
  122.0 0.8 constant_dynamic-update-slice_fusion.9
  124.3 6.8 stack.54
  131.1 21.7 %all-to-all-start = ((f32[512,1,5120]{2,1,0:T(1,128)}), f32[512,1,5120]{2,1,0:T(1,128)}, u32[]{:S(2)}, u32[]{:S(2)}) async-start(f32[512,1,5120]{2,1,0:T(1,128)} %stack.54), calls=%async_computation | async-start | bytes 20971520 | tf_op jit(solution)/shard_map/all_to_all | solution.py:173
  153.7 0.7 convolution_bitcast_fusion.9
  155.4 550.8 %all-reduce.24.cloned.1.call-done = f32[16384]{0:T(1024)} async-done(((f32[16384]{0:T(1024)}), f32[16384]{0:T(1024)}) %all-reduce.24.cloned.1.call-update) | async-done | bytes 65552
  706.2 0.9 reshape.211
  707.3 22.0 %copy.42 = f32[512,1,5120]{0,2,1:T(8,128)} copy(f32[512,1,5120]{2,1,0:T(1,128)} %all-to-all-done) | data formatting | bytes 20971520 | tf_op jit(solution)/shard_map/all_to_all | solution.py:173
  729.3 4.7 fusion.83
  734.0 1.1 multiply_reduce_fusion.18
  735.3 0.8 copy-done.2
  736.1 1.0 copy-done.3
  737.3 1.3 slice-done.2
  738.5 2.1 multiply_reduce_fusion.25
  740.7 0.7 multiply_reduce_fusion.30
  744.6 4.1 multiply_reduce_fusion.9
  748.8 6.3 multiply_reduce_fusion.16
  755.0 0.7 multiply_reduce_fusion.28
  758.9 4.1 multiply_reduce_fusion
  763.1 6.3 multiply_reduce_fusion.7
  769.4 0.7 fusion.39
  (72 shorter events, 11.0 us)
Async XLA Ops:
  7.2 1.5 copy-start
  9.1 17.8 %collective-permute-start.1 = (f32[2,2,3,128]{3,2,1,0:T(4,128)S(1)}, f32[2,2,3,128]{3,2,1,0:T(4,128)S(1)}, u32[]{:S(2)}, u32[]{:S(2)}) collective-permute-start(f32[2,2,3,128]{3,2,1,0:T(4,128)S(1)} %get-tuple-element.73), channel_id=1, source_target_pairs={{16,0},{32,16},{48,32},{64,48},{80,64},{96,80},{112,96},{128,112},... | collective-permute-start | bytes 18440 | tf_op jit(solution)/shard_map/ppermute | solution.py:28
  17.9 9.0 %collective-permute-start = (f32[2,2,3,128]{3,2,1,0:T(4,128)S(1)}, f32[2,2,3,128]{3,2,1,0:T(4,128)S(1)}, u32[]{:S(2)}, u32[]{:S(2)}) collective-permute-start(f32[2,2,3,128]{3,2,1,0:T(4,128)S(1)} %get-tuple-element.72), channel_id=1, source_target_pairs={{0,16},{16,32},{32,48},{48,64},{64,80},{80,96},{96,112},{112,128},... | collective-permute-start | bytes 18440 | tf_op jit(solution)/shard_map/ppermute | solution.py:27
  21.3 15.9 %collective-permute-start.5 = (f32[32,3,5,128]{3,0,2,1:T(8,128)S(1)}, f32[32,3,5,128]{3,0,2,1:T(8,128)S(1)}, u32[]{:S(2)}, u32[]{:S(2)}) collective-permute-start(f32[32,3,5,128]{3,0,2,1:T(8,128)S(1)} %get-tuple-element.47), channel_id=1, source_target_pairs={{16,0},{32,16},{48,32},{64,48},{80,64},{96,80},{112,96},{128,112},... | collective-permute-start | bytes 737288 | tf_op jit(solution)/shard_map/ppermute | solution.py:28
  23.7 13.5 %collective-permute-start.4 = (f32[32,3,5,128]{3,0,2,1:T(8,128)S(1)}, f32[32,3,5,128]{3,0,2,1:T(8,128)S(1)}, u32[]{:S(2)}, u32[]{:S(2)}) collective-permute-start(f32[32,3,5,128]{3,0,2,1:T(8,128)S(1)} %get-tuple-element.46), channel_id=1, source_target_pairs={{0,16},{16,32},{32,48},{48,64},{64,80},{80,96},{96,112},{112,128},... | collective-permute-start | bytes 737288 | tf_op jit(solution)/shard_map/ppermute | solution.py:27
  27.0 9.6 %collective-permute-start.3 = (f32[2,12,2,128]{3,2,1,0:T(2,128)S(1)}, f32[2,12,2,128]{3,2,1,0:T(2,128)S(1)}, u32[]{:S(2)}, u32[]{:S(2)}) collective-permute-start(f32[2,12,2,128]{3,2,1,0:T(2,128)S(1)} %get-tuple-element.71), channel_id=1, source_target_pairs={{1,0},{2,1},{3,2},{4,3},{5,4},{6,5},{7,6},{8,7},{9,8},{10,9},{11,1... | collective-permute-start | bytes 73736 | tf_op jit(solution)/shard_map/ppermute | solution.py:28
  28.3 8.9 %collective-permute-start.2 = (f32[2,12,2,128]{3,2,1,0:T(2,128)S(1)}, f32[2,12,2,128]{3,2,1,0:T(2,128)S(1)}, u32[]{:S(2)}, u32[]{:S(2)}) collective-permute-start(f32[2,12,2,128]{3,2,1,0:T(2,128)S(1)} %get-tuple-element.70), channel_id=1, source_target_pairs={{0,1},{1,2},{2,3},{3,4},{4,5},{5,6},{6,7},{7,8},{8,9},{9,10},{10,1... | collective-permute-start | bytes 73736 | tf_op jit(solution)/shard_map/ppermute | solution.py:27
  37.5 35.8 %collective-permute-start.6 = (f32[32,16,3,128]{3,0,2,1:T(8,128)S(1)}, f32[32,16,3,128]{3,0,2,1:T(8,128)S(1)}, u32[]{:S(2)}, u32[]{:S(2)}) collective-permute-start(f32[32,16,3,128]{3,0,2,1:T(8,128)S(1)} %get-tuple-element.45), channel_id=1, source_target_pairs={{0,1},{1,2},{2,3},{3,4},{4,5},{5,6},{6,7},{7,8},{8,9},{9,10},{10,1... | collective-permute-start | bytes 2359304 | tf_op jit(solution)/shard_map/ppermute | solution.py:27
  45.8 75.4 %collective-permute-start.7 = (f32[32,16,3,128]{3,0,2,1:T(8,128)S(1)}, f32[32,16,3,128]{3,0,2,1:T(8,128)S(1)}, u32[]{:S(2)}, u32[]{:S(2)}) collective-permute-start(f32[32,16,3,128]{3,0,2,1:T(8,128)S(1)} %get-tuple-element.44), channel_id=1, source_target_pairs={{1,0},{2,1},{3,2},{4,3},{5,4},{6,5},{7,6},{8,7},{9,8},{10,9},{11,1... | collective-permute-start | bytes 2359304 | tf_op jit(solution)/shard_map/ppermute | solution.py:28
  124.2 6.9 copy-start.5
  131.1 576.1 %all-to-all-start = ((f32[512,1,5120]{2,1,0:T(1,128)}), f32[512,1,5120]{2,1,0:T(1,128)}, u32[]{:S(2)}, u32[]{:S(2)}) async-start(f32[512,1,5120]{2,1,0:T(1,128)} %stack.54), calls=%async_computation | async-start | bytes 20971520 | tf_op jit(solution)/shard_map/all_to_all | solution.py:173
  152.8 553.4 %all-reduce.24.cloned.1.call-start = ((), (), s32[]{:S(2)}) async-start(), calls=%async_computation.1 | async-start | bytes 131072
  154.7 0.6 copy-start.4
  729.3 8.0 %slice-start = ((s8[10485760]{0:T(1024)(128)(4,1)}), s8[4194304]{0:T(1024)(128)(4,1)S(1)}, s32[]{:S(2)}) async-start(s8[10485760]{0:T(1024)(128)(4,1)} %bitcast.127), calls=%async_computation.2 | async-start | bytes 8388608
  729.3 8.0 %slice-start.1 = ((s8[10485760]{0:T(1024)(128)(4,1)}), s8[2097152]{0:T(1024)(128)(4,1)S(1)}, s32[]{:S(2)}) async-start(s8[10485760]{0:T(1024)(128)(4,1)} %bitcast.127), calls=%async_computation.3 | async-start | bytes 4194304
  734.0 1.3 copy-start.1
  734.0 2.1 copy-start.2
  734.0 3.1 copy-start.3
  734.0 4.5 slice-start.2
Sparse Core Ops, SparseCore 0:
  159.0 547.0 all-reduce.23
